TPU v7x, 32 devices: a whole 2x2x4 slice. The times are simulated.
32 devices in a mesh: comp: 4 (over x, core), mom: 8 (over z, y).
Axes of the slice: x: 2, y: 2, z: 4, core: 2. Of those that a mesh axis runs over, the one named last changes fastest.
Arguments:
- green_guess: float32 [4, 512, 192, 384], P('comp', 'mom'), may hold values from -3 to 3
- green_free: float32 [4, 512, 192, 384], P('comp', 'mom'), may hold values from -3 to 3
- retarded: float32 [512, 192, 384], P('mom'), may hold values from -0.3125 to 0.3125
- momentum_order: int32 [512], replicated, may hold values from 0 to 511, each once
Outputs:
- green_final: float32 [4, 512, 192, 384], P('comp', 'mom')
- self_energy: float32 [4, 512, 192, 384], P('comp', 'mom')
Inputs may be any that keep to these rules, and one draw needn't show every extreme that they name: `momentum_order`: a permutation of the lattice momenta 0 to 511.
All inputs are finite; a program needn't handle non-finite values.
Results may differ from a plain program's by a relative error of at most 0.00013.
Values sent between devices are 32-bit elements; how exact they have to be, the bound alone decides.
A program may use at most 192 MiB of HBM per device.

v0:
```python
import math

import jax
import jax.numpy as jnp
from jax import lax
from jax.sharding import PartitionSpec as P

K = 512
L1 = 16


highest = lax.Precision.HIGH


def partner(x, axis, bit):
    return lax.ppermute(x, axis, [(i, i ^ 1 << bit) for i in range(lax.axis_size(axis))])


def phase_tables(momentum_order, count, first_len):
    second_len = count // first_len
    site_ids = jnp.arange(count, dtype=jnp.int32)
    site_one = site_ids // second_len
    site_two = site_ids % second_len
    mom_one = momentum_order // second_len
    mom_two = momentum_order % second_len
    phases = (
        site_one[:, None] * mom_one[None, :] * second_len
        + site_two[:, None] * mom_two[None, :] * first_len
    ) % count
    angles = phases.astype(jnp.float32) * (2.0 * math.pi / count)
    norm_factor = 1.0 / math.sqrt(count)
    return (jnp.cos(angles) * norm_factor, jnp.sin(angles) * norm_factor)


def forward_transform(values, cosine, sine_table, half_width):
    full_shape = values.shape
    flattened = values.reshape(full_shape[0], -1)
    with_cos = jnp.dot(
        cosine, flattened, precision=highest, preferred_element_type=jnp.float32
    ).reshape(full_shape)
    with_sin = jnp.dot(
        sine_table, flattened, precision=highest, preferred_element_type=jnp.float32
    ).reshape(full_shape)
    real_part = with_cos[..., :half_width] - with_sin[..., half_width:]
    imag_part = with_cos[..., half_width:] + with_sin[..., :half_width]
    return jnp.concatenate([real_part, imag_part], axis=-1)


def inverse_transform(values, cos_back, sin_back, half_width):
    full_shape = values.shape
    flattened = values.reshape(full_shape[0], -1)
    with_cos = jnp.dot(
        cos_back, flattened, precision=highest, preferred_element_type=jnp.float32
    ).reshape(full_shape)
    with_sin = jnp.dot(
        sin_back, flattened, precision=highest, preferred_element_type=jnp.float32
    ).reshape(full_shape)
    real_part = with_cos[..., :half_width] + with_sin[..., half_width:]
    imag_part = with_cos[..., half_width:] - with_sin[..., :half_width]
    return jnp.concatenate([real_part, imag_part], axis=-1)


def triple(own_part, second, conj_factor, half_width):
    prod_real = (
        own_part[..., :half_width] * second[..., :half_width]
        - own_part[..., half_width:] * second[..., half_width:]
    )
    prod_imag = (
        own_part[..., :half_width] * second[..., half_width:]
        + own_part[..., half_width:] * second[..., :half_width]
    )
    conj_real = conj_factor[..., :half_width]
    conj_imag = conj_factor[..., half_width:]
    real_part = prod_real * conj_real + prod_imag * conj_imag
    imag_part = prod_imag * conj_real - prod_real * conj_imag
    return -jnp.concatenate([real_part, imag_part], axis=-1)


def dyson(sigma_mom, retarded, free_part, half_width):
    ret_real = retarded[..., :half_width]
    ret_imag = retarded[..., half_width:]
    swapped = jnp.concatenate([-sigma_mom[..., half_width:], sigma_mom[..., :half_width]], axis=-1)
    left_prod = jnp.einsum(
        "kij,kjx->kix", ret_real, sigma_mom, precision=highest, preferred_element_type=jnp.float32
    )
    left_prod = left_prod + jnp.einsum(
        "kij,kjx->kix", ret_imag, swapped, precision=highest, preferred_element_type=jnp.float32
    )
    turned = jnp.concatenate([left_prod[..., half_width:], -left_prod[..., :half_width]], axis=-1)
    real_part = jnp.einsum(
        "kim,kjm->kij", left_prod, retarded, precision=highest, preferred_element_type=jnp.float32
    )
    imag_part = jnp.einsum(
        "kim,kjm->kij", turned, retarded, precision=highest, preferred_element_type=jnp.float32
    )
    return free_part + jnp.concatenate([real_part, imag_part], axis=-1)


CHUNKS = 3
GROUPS = 4


def exchange(send, axis):
    size = lax.axis_size(axis)
    return [send[0]] + [
        lax.ppermute(send[s], axis, [(i, i ^ s) for i in range(size)]) for s in range(1, size)
    ]


def on_device(green_guess, green_free, retarded, momentum_order):
    mom_count = lax.axis_size("mom")
    me = lax.axis_index("mom")
    width = green_guess.shape[-1]
    half_width = width // 2
    k_local = green_guess.shape[1]
    tile_rows = half_width // mom_count
    rows = tile_rows // CHUNKS
    group = k_local // GROUPS
    cosine, sine_table = phase_tables(momentum_order, K, L1)
    cos_back = cosine.T
    sin_back = sine_table.T
    free_local = green_free[0]
    current = green_guess[0]

    tiled = current.reshape(k_local, mom_count, CHUNKS, rows, width)
    arrived = [
        lax.all_to_all(tiled[:, :, c], "mom", split_axis=1, concat_axis=0, tiled=True)
        for c in range(CHUNKS)
    ]
    pieces = []
    for c in range(CHUNKS):
        in_sites = forward_transform(arrived[c][:, 0], cosine, sine_table, half_width)
        spin_other = partner(in_sites, "comp", 1)
        cross_other = partner(spin_other, "comp", 0)
        sigma_sites = triple(in_sites, spin_other, cross_other, half_width)
        tile = inverse_transform(sigma_sites, cos_back, sin_back, half_width)
        pieces.append(lax.all_to_all(tile.reshape(mom_count, k_local, 1, rows, width), "mom", split_axis=0, concat_axis=2, tiled=True))
    sigma = jnp.stack(pieces, axis=3).reshape(k_local, half_width, width)
    return (dyson(sigma, retarded, free_local, half_width)[None], sigma[None])


def solution(mesh):
    return jax.shard_map(
        on_device,
        mesh=mesh,
        in_specs=(
            P("comp", "mom", None, None),
            P("comp", "mom", None, None),
            P("mom", None, None),
            P(),
        ),
        out_specs=(P("comp", "mom", None, None), P("comp", "mom", None, None)),
        check_vma=False,
    )
```

profile of v0, /device:TPU:0, one launch (start us, length us, event | category | flops | bytes accessed | tf_op | source)
XLA Modules:
  0.0 1086.0 jit_solution(13214193050168592810)
XLA Ops:
  0.6 12.0 %fusion.156 = (f32[64,8,1,8,384]{4,3,2,1,0:T(8,128)S(1)}, f32[64,8,1,8,384]{4,3,2,1,0:T(8,128)}, f32[64,8,1,8,384]{4,3,2,1,0:T(8,128)}) fusion(f32[64,8,3,8,384]{4,3,2,1,0:T(8,128)} %bitcast.154), kind=kLoop, calls=%fused_computation.206 | loop fusion | bytes 37748736 | tf_op jit(solution)/shard_map/slice | solution.py:127
  28.9 132.4 %all-to-all-done = f32[64,8,8,384]{3,2,0,1:T(8,128)} async-done(((f32[64,8,8,384]{3,2,0,1:T(8,128)}), f32[64,8,8,384]{3,2,0,1:T(8,128)}, u32[]{:S(2)}, u32[]{:S(2)}) %all-to-all-start) | async-done | bytes 6291488 | tf_op jit(solution)/shard_map/all_to_all | solution.py:127
  179.6 12.2 %fusion.44 = f32[512,8,384]{0,2,1:T(8,128)S(1)} fusion(f32[8,384,512]{2,1,0:T(8,128)} %bitcast.134, s32[512]{0:T(512)S(1)} %get-tuple-element.31, s32[512]{0:T(512)S(1)} %get-tuple-element.32, s32[512]{0:T(512)S(1)} %get-tuple-element.30, s32[512]{0:T(512)S(1)} %add_select_fusion.3), kind=kOutput, calls=%fused_computation.81 | convolution fusion | flops 4836818944 | bytes 12591104 | tf_op jit(solution)/shard_map/dot_general | solution.py:41
  191.9 11.6 %fusion.53 = f32[512,8,384]{0,2,1:T(8,128)} fusion(f32[8,384,512]{2,1,0:T(8,128)S(1)} %bitcast.135, s32[512]{0:T(512)S(1)} %get-tuple-element.31, s32[512]{0:T(512)S(1)} %get-tuple-element.32, s32[512]{0:T(512)S(1)} %get-tuple-element.30, s32[512]{0:T(512)S(1)} %add_select_fusion.3), kind=kOutput, calls=%fused_computation.90 | convolution fusion | flops 4836818944 | bytes 12591104 | tf_op jit(solution)/shard_map/dot_general | solution.py:38
  217.1 86.4 %all-to-all-done.2 = f32[64,8,8,384]{3,2,0,1:T(8,128)} async-done(((f32[64,8,8,384]{3,2,0,1:T(8,128)}), f32[64,8,8,384]{3,2,0,1:T(8,128)}, u32[]{:S(2)}, u32[]{:S(2)}) %all-to-all-start.2) | async-done | bytes 6291488 | tf_op jit(solution)/shard_map/all_to_all | solution.py:127
  308.2 40.7 %collective-permute-done = f32[512,8,384]{0,2,1:T(8,128)} collective-permute-done((f32[512,8,384]{0,2,1:T(8,128)}, f32[512,8,384]{0,2,1:T(8,128)}, u32[]{:S(2)}, u32[]{:S(2)}) %collective-permute-start) | collective-permute-done | bytes 6291488 | tf_op jit(solution)/shard_map/ppermute | solution.py:16
  362.9 12.2 %fusion.41 = f32[512,8,384]{0,2,1:T(8,128)S(1)} fusion(f32[8,384,512]{2,1,0:T(8,128)} %bitcast.136, s32[512]{0:T(512)S(1)} %get-tuple-element.31, s32[512]{0:T(512)S(1)} %get-tuple-element.32, s32[512]{0:T(512)S(1)} %get-tuple-element.30, s32[512]{0:T(512)S(1)} %add_select_fusion.3), kind=kOutput, calls=%fused_computation.78 | convolution fusion | flops 4836818944 | bytes 12591104 | tf_op jit(solution)/shard_map/dot_general | solution.py:41
  375.1 9.9 fusion.50
  412.7 12.2 %fusion.24 = f32[512,8,384]{0,2,1:T(8,128)} fusion(f32[512,8,192]{0,2,1:T(8,128)S(1)} %multiply_subtract_fusion.4, f32[512,8,192]{0,2,1:T(8,128)S(1)} %get-tuple-element.2, s32[512]{0:T(512)S(1)} %get-tuple-element.31, s32[512]{0:T(512)S(1)} %get-tuple-element.32, s32[512]{0:T(512)S(1)} %get-tuple-element.30, s32[512]{0:T(512)S(1)} %add_select_fusion.3), kind=kOutput, calls=%fused_computation.40 | convolution fusion | flops 4839964672 | bytes 12591104 | tf_op jit(solution)/shard_map/dot_general | solution.py:55
  450.4 79.2 %collective-permute-done.2 = f32[512,8,384]{0,2,1:T(8,128)} collective-permute-done((f32[512,8,384]{0,2,1:T(8,128)}, f32[512,8,384]{0,2,1:T(8,128)}, u32[]{:S(2)}, u32[]{:S(2)}) %collective-permute-start.2) | collective-permute-done | bytes 6291488 | tf_op jit(solution)/shard_map/ppermute | solution.py:16
  543.0 12.2 %fusion.47 = f32[512,8,384]{0,2,1:T(8,128)S(1)} fusion(f32[8,384,512]{2,1,0:T(8,128)} %bitcast.138, s32[512]{0:T(512)S(1)} %get-tuple-element.31, s32[512]{0:T(512)S(1)} %get-tuple-element.32, s32[512]{0:T(512)S(1)} %get-tuple-element.30, s32[512]{0:T(512)S(1)} %add_select_fusion.3), kind=kOutput, calls=%fused_computation.84 | convolution fusion | flops 4836818944 | bytes 12591104 | tf_op jit(solution)/shard_map/dot_general | solution.py:38
  555.2 11.9 %fusion.38 = f32[512,8,384]{0,2,1:T(8,128)} fusion(f32[8,384,512]{2,1,0:T(8,128)S(1)} %bitcast.139, s32[512]{0:T(512)S(1)} %get-tuple-element.31, s32[512]{0:T(512)S(1)} %get-tuple-element.32, s32[512]{0:T(512)S(1)} %get-tuple-element.30, s32[512]{0:T(512)S(1)} %add_select_fusion.3), kind=kOutput, calls=%fused_computation.75 | convolution fusion | flops 4836818944 | bytes 12591104 | tf_op jit(solution)/shard_map/dot_general | solution.py:41
  625.6 89.4 %collective-permute-done.4 = f32[512,8,384]{0,2,1:T(8,128)} collective-permute-done((f32[512,8,384]{0,2,1:T(8,128)}, f32[512,8,384]{0,2,1:T(8,128)}, u32[]{:S(2)}, u32[]{:S(2)}) %collective-permute-start.4) | collective-permute-done | bytes 6291488 | tf_op jit(solution)/shard_map/ppermute | solution.py:16
  715.0 10.4 collective-permute-done.5
  743.3 12.6 %fusion.16 = f32[512,8,384]{0,2,1:T(8,128)S(1)} fusion(f32[512,8,192]{0,2,1:T(8,128)} %copy-done.15, f32[512,8,192]{0,2,1:T(8,128)} %copy-done.14, s32[512]{0:T(512)S(1)} %get-tuple-element.31, s32[512]{0:T(512)S(1)} %get-tuple-element.32, s32[512]{0:T(512)S(1)} %get-tuple-element.30, s32[512]{0:T(512)S(1)} %add_select_fusion.3), kind=kOutput, calls=%fused_computation.36 | convolution fusion | flops 4839964672 | bytes 12591104 | tf_op jit(solution)/shard_map/dot_general | solution.py:55
  786.3 125.8 %all-to-all-done.5 = f32[8,64,1,8,384]{4,3,1,2,0:T(8,128)} async-done(((f32[8,64,1,8,384]{4,3,1,2,0:T(8,128)}), f32[8,64,1,8,384]{4,3,1,2,0:T(8,128)}, u32[]{:S(2)}, u32[]{:S(2)}) %all-to-all-start.5) | async-done | bytes 6291488 | tf_op jit(solution)/shard_map/all_to_all | solution.py:137
  931.0 9.9 slice_negate_fusion.1
  940.9 25.7 %fusion.9 = f32[64,384,192]{1,2,0:T(8,128)} fusion(f32[64,192,384]{2,1,0:T(8,128)} %bitcast.132, f32[64,192,384]{2,1,0:T(8,128)} %param.6), kind=kOutput, calls=%fused_computation.13 | convolution fusion | flops 5435817984 | bytes 50331648 | tf_op jit(solution)/shard_map/kij,kjx->kix/dot_general | solution.py:83
  966.6 26.0 %fusion = f32[64,384,192]{1,2,0:T(8,128)} fusion(f32[64,192,192]{2,1,0:T(8,128)} %get-tuple-element.14, f32[64,192,192]{2,1,0:T(8,128)} %get-tuple-element.13, f32[64,192,384]{2,1,0:T(8,128)} %param.6), kind=kOutput, calls=%fused_computation.1 | convolution fusion | flops 5440536576 | bytes 56623104 | tf_op jit(solution)/shard_map/kij,kjx->kix/dot_general | solution.py:86
  992.6 24.4 %fusion.28 = f32[1,64,192,192]{3,2,1,0:T(8,128)} fusion(f32[64,192,384]{2,1,0:T(8,128)} %param.6, f32[64,384,192]{1,2,0:T(8,128)} %fusion.9, f32[64,384,192]{1,2,0:T(8,128)} %fusion), kind=kOutput, calls=%fused_computation.42 | convolution fusion | flops 5440536576 | bytes 66060288 | tf_op jit(solution)/shard_map/kim,kjm->kij/dot_general | solution.py:90
  1016.9 12.5 %add_bitcast_fusion = f32[64,192,384]{2,1,0:T(8,128)S(1)} fusion(f32[64,384,192]{1,2,0:T(8,128)} %fusion.9, f32[64,384,192]{1,2,0:T(8,128)} %fusion), kind=kLoop, calls=%fused_computation.15 | loop fusion | flops 4718592 | bytes 56623104 | tf_op jit(solution)/shard_map/add | solution.py:86
  1029.4 10.0 fusion.155
  1039.5 24.0 %fusion.31 = f32[1,64,192,192]{3,2,1,0:T(8,128)} fusion(f32[64,192,384]{2,1,0:T(8,128)} %param.6, f32[64,192,192]{2,1,0:T(8,128)} %get-tuple-element.12, f32[64,192,192]{2,1,0:T(8,128)} %get-tuple-element.11), kind=kOutput, calls=%fused_computation.43 | convolution fusion | flops 5440536576 | bytes 47185920 | tf_op jit(solution)/shard_map/kim,kjm->kij/dot_general | solution.py:93
  1063.4 22.1 %maximum_add_fusion = f32[1,64,192,384]{3,2,1,0:T(8,128)} fusion(f32[1,64,192,384]{3,2,1,0:T(8,128)} %param.5, f32[1,64,192,192]{3,2,1,0:T(8,128)} %fusion.31, f32[1,64,192,192]{3,2,1,0:T(8,128)} %fusion.28), kind=kLoop, calls=%fused_computation.9 | loop fusion | flops 9437184 | bytes 56623104 | tf_op jit(solution)/shard_map/add | solution.py:96
  (96 shorter events, 258.8 us)
Async XLA Ops:
  15.8 145.5 %all-to-all-start = ((f32[64,8,8,384]{3,2,0,1:T(8,128)}), f32[64,8,8,384]{3,2,0,1:T(8,128)}, u32[]{:S(2)}, u32[]{:S(2)}) async-start(f32[64,8,8,384]{3,2,0,1:T(8,128)} %bitcast.149), calls=%async_computation | async-start | bytes 12582912 | tf_op jit(solution)/shard_map/all_to_all | solution.py:127
  161.3 142.2 %all-to-all-start.2 = ((f32[64,8,8,384]{3,2,0,1:T(8,128)}), f32[64,8,8,384]{3,2,0,1:T(8,128)}, u32[]{:S(2)}, u32[]{:S(2)}) async-start(f32[64,8,8,384]{3,2,0,1:T(8,128)} %bitcast.145), calls=%async_computation.2 | async-start | bytes 12582912 | tf_op jit(solution)/shard_map/all_to_all | solution.py:127
  179.6 12.2 %copy-start.1 = (f32[3072,512]{1,0:T(8,128)S(1)}, f32[3072,512]{1,0:T(8,128)}, u32[]{:S(2)}) copy-start(f32[3072,512]{1,0:T(8,128)} %copy.33) | copy-start | bytes 18874372
  191.8 22.2 %slice-start = ((s8[6291456]{0:T(1024)(128)(4,1)}), s8[4194304]{0:T(1024)(128)(4,1)S(1)}, s32[]{:S(2)}) async-start(s8[6291456]{0:T(1024)(128)(4,1)} %bitcast.143), calls=%async_computation.6 | async-start | bytes 8388608
  203.4 10.6 slice-start.1
  212.5 136.5 %collective-permute-start = (f32[512,8,384]{0,2,1:T(8,128)}, f32[512,8,384]{0,2,1:T(8,128)}, u32[]{:S(2)}, u32[]{:S(2)}) collective-permute-start(f32[512,8,384]{0,2,1:T(8,128)} %pad_maximum_fusion.1), channel_id=1, source_target_pairs={{0,16},{8,24},{16,0},{24,8},{1,17},{9,25},{17,1},{25,9},{2,18},{10... | collective-permute-start | bytes 18874376 | tf_op jit(solution)/shard_map/ppermute | solution.py:16
  303.5 142.0 %all-to-all-start.4 = ((f32[64,8,8,384]{3,2,0,1:T(8,128)}), f32[64,8,8,384]{3,2,0,1:T(8,128)}, u32[]{:S(2)}, u32[]{:S(2)}) async-start(f32[64,8,8,384]{3,2,0,1:T(8,128)} %bitcast.140), calls=%async_computation.4 | async-start | bytes 12582912 | tf_op jit(solution)/shard_map/all_to_all | solution.py:127
  349.0 43.9 %collective-permute-start.1 = (f32[512,8,384]{0,2,1:T(8,128)}, f32[512,8,384]{0,2,1:T(8,128)}, u32[]{:S(2)}, u32[]{:S(2)}) collective-permute-start(f32[512,8,384]{0,2,1:T(8,128)} %collective-permute-done), channel_id=1, source_target_pairs={{0,8},{8,0},{16,24},{24,16},{1,9},{9,1},{17,25},{25,17},{2,10},{10... | collective-permute-start | bytes 18874376 | tf_op jit(solution)/shard_map/ppermute | solution.py:16
  362.9 12.2 %copy-start.2 = (f32[3072,512]{1,0:T(8,128)S(1)}, f32[3072,512]{1,0:T(8,128)}, u32[]{:S(2)}) copy-start(f32[3072,512]{1,0:T(8,128)} %copy.38) | copy-start | bytes 18874372
  386.6 6.3 copy-start.10
  386.6 6.3 copy-start.12
  391.4 138.2 %collective-permute-start.2 = (f32[512,8,384]{0,2,1:T(8,128)}, f32[512,8,384]{0,2,1:T(8,128)}, u32[]{:S(2)}, u32[]{:S(2)}) collective-permute-start(f32[512,8,384]{0,2,1:T(8,128)} %pad_maximum_fusion.3), channel_id=1, source_target_pairs={{0,16},{8,24},{16,0},{24,8},{1,17},{9,25},{17,1},{25,9},{2,18},{10... | collective-permute-start | bytes 18874376 | tf_op jit(solution)/shard_map/ppermute | solution.py:16
  445.4 174.2 %all-to-all-start.1 = ((f32[8,64,1,8,384]{4,3,1,2,0:T(8,128)}), f32[8,64,1,8,384]{4,3,1,2,0:T(8,128)}, u32[]{:S(2)}, u32[]{:S(2)}) async-start(f32[8,64,1,8,384]{4,3,1,2,0:T(8,128)} %bitcast.141), calls=%async_computation.1 | async-start | bytes 12582912 | tf_op jit(solution)/shard_map/all_to_all | solution.py:137
  529.6 48.6 %collective-permute-start.3 = (f32[512,8,384]{0,2,1:T(8,128)}, f32[512,8,384]{0,2,1:T(8,128)}, u32[]{:S(2)}, u32[]{:S(2)}) collective-permute-start(f32[512,8,384]{0,2,1:T(8,128)} %collective-permute-done.2), channel_id=1, source_target_pairs={{0,8},{8,0},{16,24},{24,16},{1,9},{9,1},{17,25},{25,17},{2,10},{10... | collective-permute-start | bytes 18874376 | tf_op jit(solution)/shard_map/ppermute | solution.py:16
  543.0 12.2 %copy-start.3 = (f32[3072,512]{1,0:T(8,128)S(1)}, f32[3072,512]{1,0:T(8,128)}, u32[]{:S(2)}) copy-start(f32[3072,512]{1,0:T(8,128)} %copy.43) | copy-start | bytes 18874372
  571.6 5.1 copy-start.8
  571.6 6.6 copy-start.5
  576.7 138.2 %collective-permute-start.4 = (f32[512,8,384]{0,2,1:T(8,128)}, f32[512,8,384]{0,2,1:T(8,128)}, u32[]{:S(2)}, u32[]{:S(2)}) collective-permute-start(f32[512,8,384]{0,2,1:T(8,128)} %pad_maximum_fusion.5), channel_id=1, source_target_pairs={{0,16},{8,24},{16,0},{24,8},{1,17},{9,25},{17,1},{25,9},{2,18},{10... | collective-permute-start | bytes 18874376 | tf_op jit(solution)/shard_map/ppermute | solution.py:16
  619.7 105.6 %copy-start.7 = (f32[512,8,192]{0,2,1:T(8,128)S(1)}, f32[512,8,192]{0,2,1:T(8,128)}, u32[]{:S(2)}) copy-start(f32[512,8,192]{0,2,1:T(8,128)} %copy-done.6) | copy-start | bytes 9437188
  619.7 148.1 %all-to-all-start.3 = ((f32[8,64,1,8,384]{4,3,1,2,0:T(8,128)}), f32[8,64,1,8,384]{4,3,1,2,0:T(8,128)}, u32[]{:S(2)}, u32[]{:S(2)}) async-start(f32[8,64,1,8,384]{4,3,1,2,0:T(8,128)} %bitcast.142), calls=%async_computation.3 | async-start | bytes 12582912 | tf_op jit(solution)/shard_map/all_to_all | solution.py:137
  715.0 10.4 collective-permute-start.5
  767.8 144.3 %all-to-all-start.5 = ((f32[8,64,1,8,384]{4,3,1,2,0:T(8,128)}), f32[8,64,1,8,384]{4,3,1,2,0:T(8,128)}, u32[]{:S(2)}, u32[]{:S(2)}) async-start(f32[8,64,1,8,384]{4,3,1,2,0:T(8,128)} %bitcast.146), calls=%async_computation.5 | async-start | bytes 12582912 | tf_op jit(solution)/shard_map/all_to_all | solution.py:137
  912.1 6.5 copy-start.13
  924.1 6.9 copy-start
  (7 other events, 25.9 us)
where the time goes:
time: 1100 us; the launch traced here: 1090 us
  waiting for transfers between devices  570 us (52%)
  matrix products  232 us (21%)
  other arithmetic  128 us (12%)
  local copies, waits for them, and re-layouts  115 us (10%)
  starting transfers between devices  38.1 us (3%)
    all_to_all x3, waiting for transfers between devices, on_device(): lax.all_to_all(tiled[:, :, c], 'mom', split_axis=1, concat_axis=0, tiled=...  225 us
    ppermute x6, waiting for transfers between devices, partner(): lax.ppermute(x, axis, [(i, i ^ 1 << bit) for i in range(lax.axis_size(axi...  220 us
    all_to_all x3, waiting for transfers between devices, on_device(): lax.all_to_all(tile.reshape(mom_count, k_local, 1, rows, width), 'mom', s...  126 us
    unnamed x44, local copies, waits for them, and re-layouts  44 us
    dot_general x3, matrix products, forward_transform(): jnp.dot(sine_table, flattened, precision=highest, preferred_element_type=...  36.3 us
    dot_general x3, matrix products, inverse_transform(): jnp.dot(sin_back, flattened, precision=highest, preferred_element_type=jn...  34.5 us
    dot_general x3, matrix products, forward_transform(): jnp.dot(cosine, flattened, precision=highest, preferred_element_type=jnp....  33.7 us
    dot_general x3, matrix products, inverse_transform(): jnp.dot(cos_back, flattened, precision=highest, preferred_element_type=jn...  27.8 us
  transfers between devices with their start and end apart: 12, of which 8 were waited for; matrix products, arithmetic and copies ran while one was open for 26% of the time, Pallas kernels for 0%

commit v1 on v0

--- a/solution.py
+++ b/solution.py
@@ -1,8 +1,11 @@
+import functools
 import math
 
 import jax
 import jax.numpy as jnp
 from jax import lax
+from jax.experimental import pallas as pl
+from jax.experimental.pallas import tpu as pltpu
 from jax.sharding import PartitionSpec as P
 
 K = 512
@@ -107,7 +110,7 @@
     ]
 
 
-def on_device(green_guess, green_free, retarded, momentum_order):
+def on_device_plain(green_guess, green_free, retarded, momentum_order):
     mom_count = lax.axis_size("mom")
     me = lax.axis_index("mom")
     width = green_guess.shape[-1]
@@ -139,6 +142,405 @@
     return (dyson(sigma, retarded, free_local, half_width)[None], sigma[None])
 
 
+BF16 = jnp.bfloat16
+F32 = jnp.float32
+SUBLANES = 8
+LANES = 128
+GROUP_COUNT = 4
+MESH = pl.DeviceIdType.MESH
+
+
+def flip(index, mask, count):
+    out, bit = 0, 1
+    while bit < count:
+        part = lax.rem(lax.div(index, bit), 2)
+        out = out + bit * ((1 - part) if (mask // bit) % 2 else part)
+        bit *= 2
+    return out
+
+
+def split(value):
+    high = value.astype(BF16)
+    return high, (value - high.astype(F32)).astype(BF16)
+
+
+def mm(left, right, dims=((1,), (0,))):
+    return lax.dot_general(left, right, (dims, ((), ())), preferred_element_type=F32)
+
+
+def mm3(left, right, dims=((1,), (0,))):
+    return mm(left[0], right[0], dims) + (mm(left[0], right[1], dims) + mm(left[1], right[0], dims))
+
+
+def small_tables(momentum_order, count, first_len):
+    second_len = count // first_len
+    ids = jnp.arange(first_len + second_len, dtype=jnp.int32)[:, None]
+    mom_one = (momentum_order // second_len)[None, :]
+    mom_two = (momentum_order % second_len)[None, :]
+    phases = jnp.where(
+        ids < first_len,
+        (ids * mom_one * second_len) % count,
+        ((ids - first_len) * mom_two * first_len) % count,
+    )
+    angles = phases.astype(F32) * (2.0 * math.pi / count)
+    scale = jnp.where(ids < first_len, 1.0 / math.sqrt(count), 1.0).astype(F32)
+    return jnp.cos(angles) * scale, jnp.sin(angles) * scale
+
+
+def dyson_block(sigma, ret, free, half):
+    width = 2 * half
+    lane = lax.broadcasted_iota(jnp.int32, sigma.shape, 1)
+    sign = jnp.where(lane < half, -1.0, 1.0).astype(F32)
+    sig_pair = [jnp.concatenate(p, axis=0) for p in zip(split(sigma), split(pltpu.roll(sigma, half, 1) * sign))]
+    ret_parts = split(ret)
+    ret_pair = [jnp.concatenate(p, axis=0) for p in zip(ret_parts, split(pltpu.roll(ret, half, 1) * sign))]
+    left = mm3(ret_parts, sig_pair)
+    return free + mm3(split(left), ret_pair, ((1,), (1,)))
+
+
+def dyson_kernel(half, sig_ref, ret_ref, free_ref, green_ref, out_ref):
+    sigma = sig_ref[0]
+    out_ref[0] = sigma
+    green_ref[0] = dyson_block(sigma, ret_ref[0], free_ref[0], half)
+
+
+def dyson_call(sigma, retarded, free):
+    count, half, width = sigma.shape
+    spec = pl.BlockSpec((1, half, width), lambda k: (k, 0, 0))
+    shape = jax.ShapeDtypeStruct(sigma.shape, F32)
+    return pl.pallas_call(
+        functools.partial(dyson_kernel, half),
+        grid=(count,),
+        in_specs=[spec] * 3,
+        out_specs=(spec, spec),
+        out_shape=(shape, shape),
+        name="dyson",
+    )(sigma, retarded, free)
+
+
+def born_kernel(
+    n, chunks, first_len,
+    x_hbm, cos_ref, sin_ref,
+    recv_hbm, sig_hbm,
+    buf, site, gs, qsend, q, zhi, zlo, fwd_hi, fwd_lo, inv_hi, inv_lo,
+    fwd_send, fwd_recv, load_sem, gs_send, gs_recv, q_send, q_recv, rel_send, rel_recv, ret_send, ret_recv, own_sem, stage_sem,
+):
+    me = lax.axis_index("mom")
+    comp = lax.axis_index("comp")
+    core = lax.rem(comp, 2)
+    sibling = {"comp": comp + 1 - 2 * core}
+    across = {"comp": lax.rem(comp + 2, 4)}
+    sgn = (1 - 2 * core).astype(F32)
+    k_local, full, width = x_hbm.shape
+    half = width // 2
+    count = n * k_local
+    rows = SUBLANES
+    pairs = rows // 2
+    cols = pairs * width
+    second_len = count // first_len
+    group = k_local // GROUP_COUNT
+    masks = list(range(n // 2, n)) + list(range(1, n // 2))
+    peers = [flip(me, s, n) for s in masks]
+    hr = count // 2
+
+    barrier = pltpu.get_barrier_semaphore()
+    for peer in peers:
+        pl.semaphore_signal(barrier, inc=1, device_id={"mom": peer}, device_id_type=MESH)
+    pl.semaphore_signal(barrier, inc=1, device_id=sibling, device_id_type=MESH)
+    pl.semaphore_signal(barrier, inc=1, device_id=across, device_id_type=MESH)
+    pl.semaphore_wait(barrier, len(peers) + 2)
+
+    def row_of(device, c):
+        return pl.multiple_of((device * chunks + c) * rows, rows)
+
+    def fwd_copy(c, i):
+        return pltpu.make_async_remote_copy(
+            src_ref=x_hbm.at[:, pl.ds(row_of(peers[i], c), rows), :],
+            dst_ref=recv_hbm.at[c, pl.ds(me * k_local, k_local)],
+            send_sem=fwd_send.at[c, i], recv_sem=fwd_recv.at[c, i],
+            device_id={"mom": peers[i]}, device_id_type=MESH)
+
+    def ret_copy(c, g, i):
+        return pltpu.make_async_remote_copy(
+            src_ref=recv_hbm.at[c, pl.ds(peers[i] * k_local + g * group, group)],
+            dst_ref=sig_hbm.at[pl.ds(g * group, group), pl.ds(row_of(me, c), rows), :],
+            send_sem=ret_send.at[c, g, i], recv_sem=ret_recv.at[c, g, i],
+            device_id={"mom": peers[i]}, device_id_type=MESH)
+
+    def send_forward(c, carry):
+        for i in range(len(peers)):
+            fwd_copy(c, i).start()
+        return carry
+
+    lax.fori_loop(0, chunks, send_forward, 0)
+
+    def build(one, carry):
+        c1 = cos_ref[pl.ds(one, 1), :]
+        s1 = sin_ref[pl.ds(one, 1), :]
+        c2 = cos_ref[pl.ds(first_len, second_len), :]
+        s2 = sin_ref[pl.ds(first_len, second_len), :]
+        at = pl.ds(pl.multiple_of(one * second_len, second_len), second_len)
+        low = pl.ds(pl.multiple_of(count + one * second_len, second_len), second_len)
+        cosine = c1 * c2 - s1 * s2
+        sine = s1 * c2 + c1 * s2
+        site[0, at, 0:count] = cosine
+        site[1, at, 0:count] = sine
+        ch, cl = split(cosine)
+        sh, sl = split(sine)
+        for ref, cv, sv in ((fwd_hi, ch, sh), (fwd_lo, cl, sl)):
+            ref[at, 0:count] = cv
+            ref[at, count:2 * count] = -sv
+            ref[low, 0:count] = sv
+            ref[low, count:2 * count] = cv
+        return carry
+
+    lax.fori_loop(0, first_len, build, 0)
+
+    def turn(b, carry):
+        at = pl.ds(pl.multiple_of(b * 128, 128), 128)
+        low = pl.ds(pl.multiple_of(count + b * 128, 128), 128)
+        ch, cl = split(site[0, :, at].T)
+        sh, sl = split(site[1, :, at].T)
+        for ref, cv, sv in ((inv_hi, ch, sh), (inv_lo, cl, sl)):
+            ref[at, 0:count] = cv
+            ref[at, count:2 * count] = sv
+            ref[low, 0:count] = -sv
+            ref[low, count:2 * count] = cv
+        return carry
+
+    lax.fori_loop(0, count // 128, turn, 0)
+
+    tiles = width // LANES
+    flat = buf.reshape(tiles, count * rows, LANES)
+
+    def take(start, size):
+        return jnp.concatenate([flat[j, pl.ds(start, size, stride=rows), :] for j in range(tiles)], axis=1)
+
+    def put(start, size, value):
+        for j in range(tiles):
+            flat[j, pl.ds(start, size, stride=rows), :] = value[:, j * LANES:(j + 1) * LANES]
+
+    def lanes_of(j):
+        return pl.ds(j * LANES, LANES)
+
+
+    def chunk_step(c, carry):
+        slot = lax.rem(c, 2)
+        loads = []
+        for j in range(tiles):
+            loads.append(pltpu.make_async_copy(
+                x_hbm.at[:, pl.ds(row_of(me, c), rows), lanes_of(j)],
+                buf.at[j, pl.ds(me * k_local, k_local)], load_sem.at[n - 1, j]))
+            loads[-1].start()
+        for i in range(len(peers)):
+            fwd_copy(c, i).wait_recv()
+            at = pl.ds(peers[i] * k_local, k_local)
+            for j in range(tiles):
+                loads.append(pltpu.make_async_copy(
+                    recv_hbm.at[c, at, :, lanes_of(j)], buf.at[j, at], load_sem.at[i, j]))
+                loads[-1].start()
+        for load in loads:
+            load.wait()
+
+        kb = k_local
+
+        def stage(b, carry):
+            lane = lax.broadcasted_iota(jnp.int32, (kb, width), 1)
+            at = pl.ds(pl.multiple_of(b * kb, kb), kb)
+            low = pl.ds(pl.multiple_of(count + b * kb, kb), kb)
+            for p in range(pairs):
+                r0 = take(b * (kb * rows) + 2 * p, kb)
+                r1 = take(b * (kb * rows) + 2 * p + 1, kb)
+                re = jnp.where(lane < half, r0, pltpu.roll(r1, half, 1))
+                im = jnp.where(lane < half, pltpu.roll(r0, half, 1), r1)
+                here = pl.ds(p * width, width)
+                rh, rl = split(re)
+                ih, il = split(im)
+                zhi[at, here] = rh
+                zlo[at, here] = rl
+                zhi[low, here] = ih
+                zlo[low, here] = il
+            return carry
+
+        lax.fori_loop(0, count // kb, stage, 0)
+
+        def forward(step, carry):
+            m, t = lax.div(step, 3), lax.rem(step, 3)
+            plane, part = lax.div(m, 2), lax.rem(m, 2)
+            left = pl.ds(pl.multiple_of(m * hr, hr), hr)
+            right = pl.ds(pl.multiple_of(t * (cols // 3), cols // 3), cols // 3)
+            value = mm3((fwd_hi[left, :], fwd_lo[left, :]), (zhi[:, right], zlo[:, right]))
+            site[plane, pl.ds(pl.multiple_of(part * hr, hr), hr), right] = value
+            return carry
+
+        lax.fori_loop(0, 12, forward, 0)
+
+        mine = pl.multiple_of(core * hr, hr)
+        other = pl.multiple_of((1 - core) * hr, hr)
+        gs_copy = pltpu.make_async_remote_copy(
+            src_ref=site.at[:, pl.ds(other, hr), :], dst_ref=gs.at[slot],
+            send_sem=gs_send, recv_sem=gs_recv.at[slot], device_id=sibling, device_id_type=MESH)
+        gs_copy.start()
+        gs_copy.wait_recv()
+
+        rb = 16
+
+        def pair(b, carry):
+            here = pl.ds(pl.multiple_of(b * rb, rb), rb)
+            at = pl.ds(pl.multiple_of(mine + b * rb, rb), rb)
+            ore, oim = site[0, at, :], site[1, at, :]
+            sre, sim = gs[slot, 0, here, :], gs[slot, 1, here, :]
+            qsend[0, here, :] = ore * sre + oim * sim
+            qsend[1, here, :] = sgn * (oim * sre - ore * sim)
+            return carry
+
+        lax.fori_loop(0, hr // rb, pair, 0)
+
+        q_copy = pltpu.make_async_remote_copy(
+            src_ref=qsend, dst_ref=q.at[slot, :, pl.ds(mine, hr), :],
+            send_sem=q_send, recv_sem=q_recv.at[slot], device_id=across, device_id_type=MESH)
+        q_copy.start()
+        q_copy.wait_recv()
+        relay = pltpu.make_async_remote_copy(
+            src_ref=q.at[slot, :, pl.ds(mine, hr), :], dst_ref=q.at[slot, :, pl.ds(mine, hr), :],
+            send_sem=rel_send, recv_sem=rel_recv.at[slot], device_id=sibling, device_id_type=MESH)
+        relay.start()
+
+        def sigma_rows(base):
+            def body(b, carry):
+                at = pl.ds(pl.multiple_of(base + b * rb, rb), rb)
+                low = pl.ds(pl.multiple_of(count + base + b * rb, rb), rb)
+                gre, gim = site[0, at, :], site[1, at, :]
+                qre, qim = q[slot, 0, at, :], sgn * q[slot, 1, at, :]
+                rh, rl = split(gim * qim - gre * qre)
+                ih, il = split(-(gre * qim + gim * qre))
+                zhi[at, :] = rh
+                zlo[at, :] = rl
+                zhi[low, :] = ih
+                zlo[low, :] = il
+                return carry
+
+            lax.fori_loop(0, hr // rb, body, 0)
+
+        sigma_rows(mine)
+        relay.wait_recv()
+        sigma_rows(other)
+
+        def inverse(step, carry):
+            m, t = lax.div(step, 2), lax.rem(step, 2)
+            top = pl.ds(pl.multiple_of(m * hr, hr), hr)
+            bot = pl.ds(pl.multiple_of(count + m * hr, hr), hr)
+            right = pl.ds(pl.multiple_of(t * (2 * width), 2 * width), 2 * width)
+            z = (zhi[:, right], zlo[:, right])
+            re = mm3((inv_hi[top, :], inv_lo[top, :]), z)
+            im = mm3((inv_hi[bot, :], inv_lo[bot, :]), z)
+            lane = lax.broadcasted_iota(jnp.int32, (hr, width), 1)
+            for p in range(2):
+                rep = re[:, p * width:(p + 1) * width]
+                imp = im[:, p * width:(p + 1) * width]
+                r0 = jnp.where(lane < half, rep, pltpu.roll(imp, half, 1))
+                r1 = jnp.where(lane < half, pltpu.roll(rep, half, 1), imp)
+                base = m * (hr * rows) + t * 4 + 2 * p
+                put(base, hr, r0)
+                put(base + 1, hr, r1)
+            return carry
+
+        lax.fori_loop(0, 4, inverse, 0)
+
+        outs = []
+        for j in range(tiles):
+            outs.append(pltpu.make_async_copy(buf.at[j], recv_hbm.at[c, :, :, lanes_of(j)], stage_sem.at[j]))
+            outs.append(pltpu.make_async_copy(
+                buf.at[j, pl.ds(me * k_local, k_local)],
+                sig_hbm.at[:, pl.ds(row_of(me, c), rows), lanes_of(j)], own_sem.at[j]))
+        for out in outs:
+            out.start()
+        for out in outs:
+            out.wait()
+
+        def send_back(g, carry):
+            for i in range(len(peers)):
+                ret_copy(c, g, i).start()
+            return carry
+
+        lax.fori_loop(0, GROUP_COUNT, send_back, 0)
+        gs_copy.wait_send()
+        q_copy.wait_send()
+        relay.wait_send()
+        return carry
+
+    lax.fori_loop(0, chunks, chunk_step, 0)
+
+    def finish(c, carry):
+        for i in range(len(peers)):
+            fwd_copy(c, i).wait_send()
+
+        def inner(g, carry):
+            for i in range(len(peers)):
+                ret_copy(c, g, i).wait()
+            return carry
+
+        return lax.fori_loop(0, GROUP_COUNT, inner, carry)
+
+    lax.fori_loop(0, chunks, finish, 0)
+
+
+def born_call(n, x, cosine, sine, first_len):
+    k_local, full, width = x.shape
+    count = n * k_local
+    rows = SUBLANES
+    chunks = full // n // rows
+    cols = rows * width // 2
+    tiles = width // LANES
+    hr = count // 2
+    any_spec = pl.BlockSpec(memory_space=pl.ANY)
+    vmem = pl.BlockSpec(memory_space=pltpu.VMEM)
+    dma = pltpu.SemaphoreType.DMA
+    return pl.pallas_call(
+        functools.partial(born_kernel, n, chunks, first_len),
+        out_shape=(
+            jax.ShapeDtypeStruct((chunks, count, rows, width), F32),
+            jax.ShapeDtypeStruct(x.shape, F32),
+        ),
+        in_specs=[any_spec, vmem, vmem],
+        out_specs=(any_spec, any_spec),
+        scratch_shapes=[
+            pltpu.VMEM((tiles, count, rows, LANES), F32),
+            pltpu.VMEM((2, count, cols), F32),
+            pltpu.VMEM((2, 2, hr, cols), F32),
+            pltpu.VMEM((2, hr, cols), F32),
+            pltpu.VMEM((2, 2, count, cols), F32),
+            pltpu.VMEM((2 * count, cols), BF16),
+            pltpu.VMEM((2 * count, cols), BF16),
+            pltpu.VMEM((2 * count, 2 * count), BF16),
+            pltpu.VMEM((2 * count, 2 * count), BF16),
+            pltpu.VMEM((2 * count, 2 * count), BF16),
+            pltpu.VMEM((2 * count, 2 * count), BF16),
+            dma((chunks, n - 1)), dma((chunks, n - 1)), dma((n, tiles)),
+            dma(()), dma((2,)), dma(()), dma((2,)), dma(()), dma((2,)),
+            dma((chunks, GROUP_COUNT, n - 1)), dma((chunks, GROUP_COUNT, n - 1)),
+            dma((tiles,)), dma((tiles,)),
+        ],
+        compiler_params=pltpu.CompilerParams(
+            collective_id=0, has_side_effects=True, vmem_limit_bytes=67043328
+        ),
+        name="born",
+    )(x, cosine, sine)
+
+
+def on_device(green_guess, green_free, retarded, momentum_order):
+    n = lax.axis_size("mom")
+    k_local, full, width = green_guess.shape[1:]
+    count = n * k_local
+    fits = n & (n - 1) == 0 and full % (n * SUBLANES) == 0 and lax.axis_size("comp") == 4 and count % 512 == 0 and width % LANES == 0
+    if not fits:
+        return on_device_plain(green_guess, green_free, retarded, momentum_order)
+    cosine, sine = small_tables(momentum_order, count, L1)
+    _, sigma = born_call(n, green_guess[0], cosine, sine, L1)
+    green, sigma = dyson_call(sigma, retarded, green_free[0])
+    return green[None], sigma[None]
+
+
 def solution(mesh):
     return jax.shard_map(
         on_device,

time: 1100 us -> 925 us (0.84)
  Pallas kernels: 0 us -> 911 us
  waiting for transfers between devices: 570 us -> 0 us
  matrix products: 232 us -> 0 us
  other arithmetic: 128 us -> 1.9 us
  local copies, waits for them, and re-layouts: 115 us -> 0 us
  starting transfers between devices: 38.1 us -> 0 us
    pallas_call x0 -> x2, Pallas kernels: none -> 911 us  [the longest x1 832 us: born_call(): pl.pallas_call(functools.partial(born_kernel, n, chunks, first_len), out_...]
    all_to_all x6 -> x0, waiting for transfers between devices: 351 us -> none  [the longest x3 225 us: on_device(): lax.all_to_all(tiled[:, :, c], 'mom', split_axis=1, concat_axis=0, tiled=...]
    dot_general x16 -> x0, matrix products: 232 us -> none  [the longest x3 36.3 us: forward_transform(): jnp.dot(sine_table, flattened, precision=highest, preferred_element_type=...]
    ppermute x6 -> x0, waiting for transfers between devices: 220 us -> none  [partner(): lax.ppermute(x, axis, [(i, i ^ 1 << bit) for i in range(lax.axis_size(axi...]
    add x8 -> x0, other arithmetic: 60.2 us -> none  [the longest x1 22.1 us: dyson(): return free_part + jnp.concatenate([real_part, imag_part], axis=-1)]
    unnamed x44 -> x0, local copies, waits for them, and re-layouts: 44 us -> none
    all_to_all x6 -> x0, starting transfers between devices: 33.6 us -> none  [the longest x3 16.9 us: on_device(): lax.all_to_all(tiled[:, :, c], 'mom', split_axis=1, concat_axis=0, tiled=...]
    concatenate x6 -> x0, other arithmetic: 21.8 us -> none  [the longest x3 11.6 us: forward_transform(): return jnp.concatenate([real_part, imag_part], axis=-1)]
  transfers between devices with their start and end apart: 12 -> 0, of which waited for: 8 -> 0; matrix products, arithmetic and copies ran while one was open for 26% -> 0% of each run, Pallas kernels for 0% -> 0%
where the time goes in v1:
time: 925 us; the launch traced here: 914 us
  Pallas kernels  911 us (98%)
    pallas_call x1, Pallas kernels, born_call(): pl.pallas_call(functools.partial(born_kernel, n, chunks, first_len), out_...  832 us
    pallas_call x1, Pallas kernels, dyson_call(): pl.pallas_call(functools.partial(dyson_kernel, half), grid=(count,), in_s...  79.2 us

profile of v1, /device:TPU:0, one launch (start us, length us, event | category | flops | bytes accessed | tf_op | source)
XLA Modules:
  0.0 913.7 jit_solution(1473993325887030744)
XLA Ops:
  0.7 0.7 add_select_fusion.3
  1.4 1.2 sine_multiply_fusion
  2.6 831.9 %born.1 = (f32[3,512,8,384]{3,2,1,0:T(8,128)}, f32[64,192,384]{2,1,0:T(8,128)}) custom-call(f32[64,192,384]{2,1,0:T(8,128)} %bitcast.5, f32[48,512]{1,0:T(8,128)} %get-tuple-element.9.cos_ref, f32[48,512]{1,0:T(8,128)} %get-tuple-element.8.sin_ref), custom_call_target="tpu_custom_call" | custom-call | tf_op jit(solution)/shard_map/born/pallas_call | solution.py:499
  834.4 79.2 %dyson.1 = (f32[64,192,384]{2,1,0:T(8,128)}, f32[64,192,384]{2,1,0:T(8,128)}) custom-call(f32[64,192,384]{2,1,0:T(8,128)} %get-tuple-element.5.sig_ref, f32[64,192,384]{2,1,0:T(8,128)} %ret_ref.1, f32[64,192,384]{2,1,0:T(8,128)} %bitcast.4), custom_call_target="tpu_custom_call" | custom-call | tf_op jit(solution)/shard_map/dyson/pallas_call | solution.py:211
  (3 shorter events, 0.0 us)

commit v2 on v1

--- a/solution.py
+++ b/solution.py
@@ -146,7 +146,7 @@
 F32 = jnp.float32
 SUBLANES = 8
 LANES = 128
-GROUP_COUNT = 4
+LATE_SHARE = 8
 MESH = pl.DeviceIdType.MESH
 
 
@@ -187,43 +187,85 @@
     return jnp.cos(angles) * scale, jnp.sin(angles) * scale
 
 
-def dyson_block(sigma, ret, free, half):
-    width = 2 * half
+def stacked(left, right, dims=((1,), (0,))):
+    size = left[0].shape[0]
+    both = mm(jnp.concatenate(left, axis=0), right[0], dims)
+    return both[:size] + (both[size:] + mm(left[0], right[1], dims))
+
+
+def dyson_block(sigma, ret, free):
+    half = sigma.shape[0]
     lane = lax.broadcasted_iota(jnp.int32, sigma.shape, 1)
     sign = jnp.where(lane < half, -1.0, 1.0).astype(F32)
+    ret_parts = split(ret)
     sig_pair = [jnp.concatenate(p, axis=0) for p in zip(split(sigma), split(pltpu.roll(sigma, half, 1) * sign))]
-    ret_parts = split(ret)
     ret_pair = [jnp.concatenate(p, axis=0) for p in zip(ret_parts, split(pltpu.roll(ret, half, 1) * sign))]
-    left = mm3(ret_parts, sig_pair)
-    return free + mm3(split(left), ret_pair, ((1,), (1,)))
-
-
-def dyson_kernel(half, sig_ref, ret_ref, free_ref, green_ref, out_ref):
-    sigma = sig_ref[0]
-    out_ref[0] = sigma
-    green_ref[0] = dyson_block(sigma, ret_ref[0], free_ref[0], half)
-
-
-def dyson_call(sigma, retarded, free):
-    count, half, width = sigma.shape
-    spec = pl.BlockSpec((1, half, width), lambda k: (k, 0, 0))
-    shape = jax.ShapeDtypeStruct(sigma.shape, F32)
+    left = stacked(ret_parts, sig_pair)
+    return free + stacked(split(left), ret_pair, ((1,), (1,)))
+
+
+def dyson_early_kernel(sig_ref, ret_ref, free_ref, green_ref, out_ref):
+    for i in range(sig_ref.shape[0]):
+        sigma = sig_ref[i]
+        out_ref[i] = sigma
+        green_ref[i] = dyson_block(sigma, ret_ref[i], free_ref[i])
+
+
+def dyson_late_kernel(sig_ref, ret_ref, free_ref, _green, _out, green_ref, out_ref):
+    step = ret_ref.shape[0]
+    for i in range(step):
+        sigma = sig_ref[:, pl.program_id(0) * step + i].reshape(ret_ref.shape[1:])
+        out_ref[i] = sigma
+        green_ref[i] = dyson_block(sigma, ret_ref[i], free_ref[i])
+
+
+def dyson_cost(count, half):
+    return pl.CostEstimate(
+        flops=count * half * half * half * 8 * 6, bytes_accessed=count * half * half * 2 * 4 * 5, transcendentals=0)
+
+
+def dyson_early(sigma, retarded, free):
+    early, half, width = sigma.shape
+    step = math.gcd(early, 4)
+    spec = pl.BlockSpec((step, half, width), lambda k: (k, 0, 0))
+    shape = jax.ShapeDtypeStruct(free.shape, F32)
     return pl.pallas_call(
-        functools.partial(dyson_kernel, half),
-        grid=(count,),
+        dyson_early_kernel,
+        grid=(early // step,),
         in_specs=[spec] * 3,
         out_specs=(spec, spec),
         out_shape=(shape, shape),
-        name="dyson",
+        cost_estimate=dyson_cost(early, half),
+        name="dyson_early",
     )(sigma, retarded, free)
+
+
+def dyson_late(pieces, retarded, free, green, sigma):
+    late = pieces.shape[1]
+    k_local, half, width = free.shape
+    early = k_local - late
+    step = math.gcd(math.gcd(early, late), 2)
+    spec = pl.BlockSpec((step, half, width), lambda k: (early // step + k, 0, 0))
+    any_spec = pl.BlockSpec(memory_space=pl.ANY)
+    shape = jax.ShapeDtypeStruct(free.shape, F32)
+    return pl.pallas_call(
+        dyson_late_kernel,
+        grid=(late // step,),
+        in_specs=[pl.BlockSpec(memory_space=pltpu.VMEM), spec, spec, any_spec, any_spec],
+        out_specs=(spec, spec),
+        out_shape=(shape, shape),
+        input_output_aliases={3: 0, 4: 1},
+        cost_estimate=dyson_cost(late, half),
+        name="dyson_late",
+    )(pieces, retarded, free, green, sigma)
 
 
 def born_kernel(
     n, chunks, first_len,
     x_hbm, cos_ref, sin_ref,
-    recv_hbm, sig_hbm,
+    recv_hbm, sig_hbm, late_hbm,
     buf, site, gs, qsend, q, zhi, zlo, fwd_hi, fwd_lo, inv_hi, inv_lo,
-    fwd_send, fwd_recv, load_sem, gs_send, gs_recv, q_send, q_recv, rel_send, rel_recv, ret_send, ret_recv, own_sem, stage_sem,
+    fwd_send, fwd_recv, load_sem, gs_send, gs_recv, q_send, q_recv, rel_send, rel_recv, ret_send, ret_recv, own_sem, stage_sem, late_sem,
 ):
     me = lax.axis_index("mom")
     comp = lax.axis_index("comp")
@@ -238,7 +280,8 @@
     pairs = rows // 2
     cols = pairs * width
     second_len = count // first_len
-    group = k_local // GROUP_COUNT
+    early = sig_hbm.shape[0]
+    late = k_local - early
     masks = list(range(n // 2, n)) + list(range(1, n // 2))
     peers = [flip(me, s, n) for s in masks]
     hr = count // 2
@@ -260,11 +303,11 @@
             send_sem=fwd_send.at[c, i], recv_sem=fwd_recv.at[c, i],
             device_id={"mom": peers[i]}, device_id_type=MESH)
 
-    def ret_copy(c, g, i):
+    def ret_copy(c, i):
         return pltpu.make_async_remote_copy(
-            src_ref=recv_hbm.at[c, pl.ds(peers[i] * k_local + g * group, group)],
-            dst_ref=sig_hbm.at[pl.ds(g * group, group), pl.ds(row_of(me, c), rows), :],
-            send_sem=ret_send.at[c, g, i], recv_sem=ret_recv.at[c, g, i],
+            src_ref=recv_hbm.at[c, pl.ds(peers[i] * k_local, early)],
+            dst_ref=sig_hbm.at[:, pl.ds(row_of(me, c), rows), :],
+            send_sem=ret_send.at[c, i], recv_sem=ret_recv.at[c, i],
             device_id={"mom": peers[i]}, device_id_type=MESH)
 
     def send_forward(c, carry):
@@ -312,6 +355,7 @@
 
     tiles = width // LANES
     flat = buf.reshape(tiles, count * rows, LANES)
+    by_owner = buf.reshape(tiles, n, k_local, rows, LANES)
 
     def take(start, size):
         return jnp.concatenate([flat[j, pl.ds(start, size, stride=rows), :] for j in range(tiles)], axis=1)
@@ -451,19 +495,18 @@
         for j in range(tiles):
             outs.append(pltpu.make_async_copy(buf.at[j], recv_hbm.at[c, :, :, lanes_of(j)], stage_sem.at[j]))
             outs.append(pltpu.make_async_copy(
-                buf.at[j, pl.ds(me * k_local, k_local)],
+                buf.at[j, pl.ds(me * k_local, early)],
                 sig_hbm.at[:, pl.ds(row_of(me, c), rows), lanes_of(j)], own_sem.at[j]))
+            outs.append(pltpu.make_async_copy(
+                by_owner.at[j, :, pl.ds(early, late)],
+                late_hbm.at[:, :, pl.ds(pl.multiple_of(c * rows, rows), rows), lanes_of(j)], late_sem.at[j]))
         for out in outs:
             out.start()
         for out in outs:
             out.wait()
 
-        def send_back(g, carry):
-            for i in range(len(peers)):
-                ret_copy(c, g, i).start()
-            return carry
-
-        lax.fori_loop(0, GROUP_COUNT, send_back, 0)
+        for i in range(len(peers)):
+            ret_copy(c, i).start()
         gs_copy.wait_send()
         q_copy.wait_send()
         relay.wait_send()
@@ -474,13 +517,8 @@
     def finish(c, carry):
         for i in range(len(peers)):
             fwd_copy(c, i).wait_send()
-
-        def inner(g, carry):
-            for i in range(len(peers)):
-                ret_copy(c, g, i).wait()
-            return carry
-
-        return lax.fori_loop(0, GROUP_COUNT, inner, carry)
+            ret_copy(c, i).wait()
+        return carry
 
     lax.fori_loop(0, chunks, finish, 0)
 
@@ -493,6 +531,7 @@
     cols = rows * width // 2
     tiles = width // LANES
     hr = count // 2
+    late = k_local // LATE_SHARE
     any_spec = pl.BlockSpec(memory_space=pl.ANY)
     vmem = pl.BlockSpec(memory_space=pltpu.VMEM)
     dma = pltpu.SemaphoreType.DMA
@@ -500,10 +539,11 @@
         functools.partial(born_kernel, n, chunks, first_len),
         out_shape=(
             jax.ShapeDtypeStruct((chunks, count, rows, width), F32),
-            jax.ShapeDtypeStruct(x.shape, F32),
+            jax.ShapeDtypeStruct((k_local - late, full, width), F32),
+            jax.ShapeDtypeStruct((n, late, full // n, width), F32),
         ),
         in_specs=[any_spec, vmem, vmem],
-        out_specs=(any_spec, any_spec),
+        out_specs=(any_spec, any_spec, any_spec),
         scratch_shapes=[
             pltpu.VMEM((tiles, count, rows, LANES), F32),
             pltpu.VMEM((2, count, cols), F32),
@@ -518,8 +558,8 @@
             pltpu.VMEM((2 * count, 2 * count), BF16),
             dma((chunks, n - 1)), dma((chunks, n - 1)), dma((n, tiles)),
             dma(()), dma((2,)), dma(()), dma((2,)), dma(()), dma((2,)),
-            dma((chunks, GROUP_COUNT, n - 1)), dma((chunks, GROUP_COUNT, n - 1)),
-            dma((tiles,)), dma((tiles,)),
+            dma((chunks, n - 1)), dma((chunks, n - 1)),
+            dma((tiles,)), dma((tiles,)), dma((tiles,)),
         ],
         compiler_params=pltpu.CompilerParams(
             collective_id=0, has_side_effects=True, vmem_limit_bytes=67043328
@@ -532,12 +572,14 @@
     n = lax.axis_size("mom")
     k_local, full, width = green_guess.shape[1:]
     count = n * k_local
-    fits = n & (n - 1) == 0 and full % (n * SUBLANES) == 0 and lax.axis_size("comp") == 4 and count % 512 == 0 and width % LANES == 0
+    fits = n & (n - 1) == 0 and full % (n * SUBLANES) == 0 and lax.axis_size("comp") == 4 and count % 512 == 0 and width % LANES == 0 and k_local % LATE_SHARE == 0
     if not fits:
         return on_device_plain(green_guess, green_free, retarded, momentum_order)
     cosine, sine = small_tables(momentum_order, count, L1)
-    _, sigma = born_call(n, green_guess[0], cosine, sine, L1)
-    green, sigma = dyson_call(sigma, retarded, green_free[0])
+    _, sigma, late = born_call(n, green_guess[0], cosine, sine, L1)
+    pieces = lax.all_to_all(late, "mom", split_axis=0, concat_axis=0, tiled=True)
+    green, sigma = dyson_early(sigma, retarded, green_free[0])
+    green, sigma = dyson_late(pieces, retarded, green_free[0], green, sigma)
     return green[None], sigma[None]
 
 

time: 925 us -> 874 us (0.945); the launches traced: 914 us -> 874 us
  Pallas kernels: 911 us -> 830 us
  starting transfers between devices: 0 us -> 30.3 us
  waiting for transfers between devices: 0 us -> 9.9 us
    pallas_call x1, Pallas kernels: 832 us -> 777 us  [born_call(): pl.pallas_call(functools.partial(born_kernel, n, chunks, first_len), out_...]
    all_to_all x0 -> x1, starting transfers between devices: none -> 30.3 us  [on_device(): lax.all_to_all(late, 'mom', split_axis=0, concat_axis=0, tiled=True)]
    pallas_call x1 -> x2, Pallas kernels: 79.2 us -> 52.8 us  [the longest x1 43.4 us: dyson_early(): pl.pallas_call(dyson_early_kernel, grid=(early // step,), in_specs=[spec]...]
    all_to_all x0 -> x1, waiting for transfers between devices: none -> 9.9 us  [on_device(): lax.all_to_all(late, 'mom', split_axis=0, concat_axis=0, tiled=True)]
  transfers between devices with their start and end apart: 0 -> 1, of which waited for: 0 -> 1; matrix products, arithmetic and copies ran while one was open for 0% -> 0% of each run, Pallas kernels for 0% -> 5%
where the time goes in v2:
time: 874 us
  Pallas kernels  830 us (95%)
  starting transfers between devices  30.3 us (3%)
  waiting for transfers between devices  9.9 us (1%)
    pallas_call x1, Pallas kernels, born_call(): pl.pallas_call(functools.partial(born_kernel, n, chunks, first_len), out_...  777 us
    pallas_call x1, Pallas kernels, dyson_early(): pl.pallas_call(dyson_early_kernel, grid=(early // step,), in_specs=[spec]...  43.4 us
    all_to_all x1, starting transfers between devices, on_device(): lax.all_to_all(late, 'mom', split_axis=0, concat_axis=0, tiled=True)  30.3 us
  transfers between devices with their start and end apart: 1, of which 1 were waited for; matrix products, arithmetic and copies ran while one was open for 0% of the time, Pallas kernels for 5%

profile of v2, /device:TPU:0, one launch (start us, length us, event | category | flops | bytes accessed | tf_op | source)
XLA Modules:
  0.0 873.7 jit_solution(14358014909132895428)
XLA Ops:
  0.7 0.7 add_select_fusion.3
  1.4 1.2 sine_multiply_fusion
  2.6 776.7 %born.1 = (f32[3,512,8,384]{3,2,1,0:T(8,128)}, f32[56,192,384]{2,1,0:T(8,128)}, f32[8,8,24,384]{3,2,1,0:T(8,128)}) custom-call(f32[64,192,384]{2,1,0:T(8,128)} %bitcast.4, f32[48,512]{1,0:T(8,128)} %get-tuple-element.15.cos_ref, f32[48,512]{1,0:T(8,128)} %get-tuple-element.14.sin_ref), custom_call_target="tpu_custom_call" | custom-call | tf_op jit(solution)/shard_map/born/pallas_call | solution.py:538
  779.3 30.3 %all-to-all-start = ((f32[8,8,24,384]{3,2,1,0:T(8,128)}), f32[8,8,24,384]{3,2,1,0:T(8,128)S(1)}, u32[]{:S(2)}, u32[]{:S(2)}) async-start(f32[8,8,24,384]{3,2,1,0:T(8,128)} %get-tuple-element.8), calls=%async_computation | async-start | bytes 4718592 | tf_op jit(solution)/shard_map/all_to_all | solution.py:580
  809.6 43.4 %dyson_early.1 = (f32[64,192,384]{2,1,0:T(8,128)}, f32[64,192,384]{2,1,0:T(8,128)}) custom-call(f32[56,192,384]{2,1,0:T(8,128)} %get-tuple-element.9.sig_ref, f32[64,192,384]{2,1,0:T(8,128)} %ret_ref.3, f32[64,192,384]{2,1,0:T(8,128)} %bitcast.5), custom_call_target="tpu_custom_call" | custom-call | flops 19025362944 | bytes 82575360 | tf_op jit(solution)/shard_map/dyson_early/pallas_call | solution.py:232
  853.0 9.9 %all-to-all-done.sig_ref = f32[8,8,24,384]{3,2,1,0:T(8,128)S(1)} async-done(((f32[8,8,24,384]{3,2,1,0:T(8,128)}), f32[8,8,24,384]{3,2,1,0:T(8,128)S(1)}, u32[]{:S(2)}, u32[]{:S(2)}) %all-to-all-start) | async-done | bytes 2359328 | tf_op jit(solution)/shard_map/all_to_all | solution.py:580
  862.9 0.0 copy-start
  862.9 1.4 copy-done
  864.3 9.4 %dyson_late.1 = (f32[64,192,384]{2,1,0:T(8,128)}, f32[64,192,384]{2,1,0:T(8,128)}) custom-call(f32[8,8,24,384]{3,2,1,0:T(8,128)} %copy-done, f32[64,192,384]{2,1,0:T(8,128)} %ret_ref.3, f32[64,192,384]{2,1,0:T(8,128)} %bitcast.6, f32[64,192,384]{2,1,0:T(8,128)} %get-tuple-element.10._green, ...), custom_call_target="tpu_custom_call", output_to_operand_aliasing={{0}: (3, {}), {1}: (4, {})} | custom-call | flops 2717908992 | bytes 11796480 | tf_op jit(solution)/shard_map/dyson_late/pallas_call | solution.py:251
  (3 shorter events, 0.0 us)
Async XLA Ops:
  779.3 83.6 %all-to-all-start = ((f32[8,8,24,384]{3,2,1,0:T(8,128)}), f32[8,8,24,384]{3,2,1,0:T(8,128)S(1)}, u32[]{:S(2)}, u32[]{:S(2)}) async-start(f32[8,8,24,384]{3,2,1,0:T(8,128)} %get-tuple-element.8), calls=%async_computation | async-start | bytes 4718592 | tf_op jit(solution)/shard_map/all_to_all | solution.py:580
  862.9 1.4 copy-start

commit v3 on v2

--- a/solution.py
+++ b/solution.py
@@ -153,10 +153,18 @@
 def flip(index, mask, count):
     out, bit = 0, 1
     while bit < count:
-        part = lax.rem(lax.div(index, bit), 2)
-        out = out + bit * ((1 - part) if (mask // bit) % 2 else part)
+        part, turn = lax.rem(lax.div(index, bit), 2), lax.rem(lax.div(mask, bit), 2)
+        out = out + bit * (part + turn - 2 * part * turn)
         bit *= 2
     return out
+
+
+def send_orders(count):
+    up, half = [], count // 2
+    while half:
+        up += range(half, 2 * half)
+        half //= 2
+    return up, list(range(count - 1, 0, -1))
 
 
 def split(value):
@@ -282,8 +290,7 @@
     second_len = count // first_len
     early = sig_hbm.shape[0]
     late = k_local - early
-    masks = list(range(n // 2, n)) + list(range(1, n // 2))
-    peers = [flip(me, s, n) for s in masks]
+    peers = [flip(me, a + core * (b - a), n) for a, b in zip(*send_orders(n))]
     hr = count // 2
 
     barrier = pltpu.get_barrier_semaphore()

time: 874 us -> 841 us (0.962)
  Pallas kernels: 830 us -> 795 us
    pallas_call x1, Pallas kernels: 777 us -> 743 us  [born_call(): pl.pallas_call(functools.partial(born_kernel, n, chunks, first_len), out_...]
where the time goes in v3:
time: 841 us; the launch traced here: 840 us
  Pallas kernels  795 us (95%)
  starting transfers between devices  31.5 us (4%)
  waiting for transfers between devices  9.42 us (1%)
    pallas_call x1, Pallas kernels, born_call(): pl.pallas_call(functools.partial(born_kernel, n, chunks, first_len), out_...  743 us
    pallas_call x1, Pallas kernels, dyson_early(): pl.pallas_call(dyson_early_kernel, grid=(early // step,), in_specs=[spec]...  43.4 us
    all_to_all x1, starting transfers between devices, on_device(): lax.all_to_all(late, 'mom', split_axis=0, concat_axis=0, tiled=True)  31.5 us
  transfers between devices with their start and end apart: 1, of which 1 were waited for; matrix products, arithmetic and copies ran while one was open for 0% of the time, Pallas kernels for 5%

profile of v3, /device:TPU:0, one launch (start us, length us, event | category | flops | bytes accessed | tf_op | source)
XLA Modules:
  0.0 840.3 jit_solution(1848912987965638362)
XLA Ops:
  0.7 0.7 add_select_fusion.3
  1.4 1.2 sine_multiply_fusion
  2.6 742.6 %born.1 = (f32[3,512,8,384]{3,2,1,0:T(8,128)}, f32[56,192,384]{2,1,0:T(8,128)}, f32[8,8,24,384]{3,2,1,0:T(8,128)}) custom-call(f32[64,192,384]{2,1,0:T(8,128)} %bitcast.4, f32[48,512]{1,0:T(8,128)} %get-tuple-element.15.cos_ref, f32[48,512]{1,0:T(8,128)} %get-tuple-element.14.sin_ref), custom_call_target="tpu_custom_call" | custom-call | tf_op jit(solution)/shard_map/born/pallas_call | solution.py:545
  745.2 31.5 %all-to-all-start = ((f32[8,8,24,384]{3,2,1,0:T(8,128)}), f32[8,8,24,384]{3,2,1,0:T(8,128)S(1)}, u32[]{:S(2)}, u32[]{:S(2)}) async-start(f32[8,8,24,384]{3,2,1,0:T(8,128)} %get-tuple-element.8), calls=%async_computation | async-start | bytes 4718592 | tf_op jit(solution)/shard_map/all_to_all | solution.py:587
  776.7 43.4 %dyson_early.1 = (f32[64,192,384]{2,1,0:T(8,128)}, f32[64,192,384]{2,1,0:T(8,128)}) custom-call(f32[56,192,384]{2,1,0:T(8,128)} %get-tuple-element.9.sig_ref, f32[64,192,384]{2,1,0:T(8,128)} %ret_ref.3, f32[64,192,384]{2,1,0:T(8,128)} %bitcast.5), custom_call_target="tpu_custom_call" | custom-call | flops 19025362944 | bytes 82575360 | tf_op jit(solution)/shard_map/dyson_early/pallas_call | solution.py:240
  820.1 9.4 %all-to-all-done.sig_ref = f32[8,8,24,384]{3,2,1,0:T(8,128)S(1)} async-done(((f32[8,8,24,384]{3,2,1,0:T(8,128)}), f32[8,8,24,384]{3,2,1,0:T(8,128)S(1)}, u32[]{:S(2)}, u32[]{:S(2)}) %all-to-all-start) | async-done | bytes 2359328 | tf_op jit(solution)/shard_map/all_to_all | solution.py:587
  829.5 0.0 copy-start
  829.5 1.4 copy-done
  830.9 9.4 %dyson_late.1 = (f32[64,192,384]{2,1,0:T(8,128)}, f32[64,192,384]{2,1,0:T(8,128)}) custom-call(f32[8,8,24,384]{3,2,1,0:T(8,128)} %copy-done, f32[64,192,384]{2,1,0:T(8,128)} %ret_ref.3, f32[64,192,384]{2,1,0:T(8,128)} %bitcast.6, f32[64,192,384]{2,1,0:T(8,128)} %get-tuple-element.10._green, ...), custom_call_target="tpu_custom_call", output_to_operand_aliasing={{0}: (3, {}), {1}: (4, {})} | custom-call | flops 2717908992 | bytes 11796480 | tf_op jit(solution)/shard_map/dyson_late/pallas_call | solution.py:259
  (3 shorter events, 0.0 us)
Async XLA Ops:
  745.2 84.3 %all-to-all-start = ((f32[8,8,24,384]{3,2,1,0:T(8,128)}), f32[8,8,24,384]{3,2,1,0:T(8,128)S(1)}, u32[]{:S(2)}, u32[]{:S(2)}) async-start(f32[8,8,24,384]{3,2,1,0:T(8,128)} %get-tuple-element.8), calls=%async_computation | async-start | bytes 4718592 | tf_op jit(solution)/shard_map/all_to_all | solution.py:587
  829.5 1.4 copy-start

commit v4 on v3

--- a/solution.py
+++ b/solution.py
@@ -147,6 +147,7 @@
 SUBLANES = 8
 LANES = 128
 LATE_SHARE = 8
+LATE_VMEM = 36 << 20
 MESH = pl.DeviceIdType.MESH
 
 
@@ -180,16 +181,15 @@
     return mm(left[0], right[0], dims) + (mm(left[0], right[1], dims) + mm(left[1], right[0], dims))
 
 
-def small_tables(momentum_order, count, first_len):
+def small_tables(order, count, first_len):
     second_len = count // first_len
-    ids = jnp.arange(first_len + second_len, dtype=jnp.int32)[:, None]
-    mom_one = (momentum_order // second_len)[None, :]
-    mom_two = (momentum_order % second_len)[None, :]
+    shift = second_len.bit_length() - 1
+    ids = lax.broadcasted_iota(jnp.int32, (first_len + second_len, count), 0)
+    one = lax.shift_right_logical(order, jnp.full_like(order, shift))
+    two = order & (second_len - 1)
     phases = jnp.where(
-        ids < first_len,
-        (ids * mom_one * second_len) % count,
-        ((ids - first_len) * mom_two * first_len) % count,
-    )
+        ids < first_len, ids * one * second_len, (ids - first_len) * two * first_len
+    ) & (count - 1)
     angles = phases.astype(F32) * (2.0 * math.pi / count)
     scale = jnp.where(ids < first_len, 1.0 / math.sqrt(count), 1.0).astype(F32)
     return jnp.cos(angles) * scale, jnp.sin(angles) * scale
@@ -256,6 +256,7 @@
     spec = pl.BlockSpec((step, half, width), lambda k: (early // step + k, 0, 0))
     any_spec = pl.BlockSpec(memory_space=pl.ANY)
     shape = jax.ShapeDtypeStruct(free.shape, F32)
+    pieces = pltpu.with_memory_space_constraint(pieces, pltpu.VMEM)
     return pl.pallas_call(
         dyson_late_kernel,
         grid=(late // step,),
@@ -264,15 +265,16 @@
         out_shape=(shape, shape),
         input_output_aliases={3: 0, 4: 1},
         cost_estimate=dyson_cost(late, half),
+        compiler_params=pltpu.CompilerParams(vmem_limit_bytes=LATE_VMEM),
         name="dyson_late",
     )(pieces, retarded, free, green, sigma)
 
 
 def born_kernel(
     n, chunks, first_len,
-    x_hbm, cos_ref, sin_ref,
+    x_hbm, order_ref,
     recv_hbm, sig_hbm, late_hbm,
-    buf, site, gs, qsend, q, zhi, zlo, fwd_hi, fwd_lo, inv_hi, inv_lo,
+    cos_ref, sin_ref, buf, site, gs, qsend, q, zhi, zlo, fwd_hi, fwd_lo, inv_hi, inv_lo,
     fwd_send, fwd_recv, load_sem, gs_send, gs_recv, q_send, q_recv, rel_send, rel_recv, ret_send, ret_recv, own_sem, stage_sem, late_sem,
 ):
     me = lax.axis_index("mom")
@@ -324,6 +326,8 @@
 
     lax.fori_loop(0, chunks, send_forward, 0)
 
+    cos_ref[...], sin_ref[...] = small_tables(order_ref[...], count, first_len)
+
     def build(one, carry):
         c1 = cos_ref[pl.ds(one, 1), :]
         s1 = sin_ref[pl.ds(one, 1), :]
@@ -530,7 +534,7 @@
     lax.fori_loop(0, chunks, finish, 0)
 
 
-def born_call(n, x, cosine, sine, first_len):
+def born_call(n, x, order, first_len):
     k_local, full, width = x.shape
     count = n * k_local
     rows = SUBLANES
@@ -549,9 +553,11 @@
             jax.ShapeDtypeStruct((k_local - late, full, width), F32),
             jax.ShapeDtypeStruct((n, late, full // n, width), F32),
         ),
-        in_specs=[any_spec, vmem, vmem],
+        in_specs=[any_spec, vmem],
         out_specs=(any_spec, any_spec, any_spec),
         scratch_shapes=[
+            pltpu.VMEM((first_len + count // first_len, count), F32),
+            pltpu.VMEM((first_len + count // first_len, count), F32),
             pltpu.VMEM((tiles, count, rows, LANES), F32),
             pltpu.VMEM((2, count, cols), F32),
             pltpu.VMEM((2, 2, hr, cols), F32),
@@ -572,18 +578,17 @@
             collective_id=0, has_side_effects=True, vmem_limit_bytes=67043328
         ),
         name="born",
-    )(x, cosine, sine)
+    )(x, order)
 
 
 def on_device(green_guess, green_free, retarded, momentum_order):
     n = lax.axis_size("mom")
     k_local, full, width = green_guess.shape[1:]
     count = n * k_local
-    fits = n & (n - 1) == 0 and full % (n * SUBLANES) == 0 and lax.axis_size("comp") == 4 and count % 512 == 0 and width % LANES == 0 and k_local % LATE_SHARE == 0
+    fits = n & (n - 1) == 0 and count & (count - 1) == 0 and full % (n * SUBLANES) == 0 and lax.axis_size("comp") == 4 and count % 512 == 0 and width % LANES == 0 and k_local % LATE_SHARE == 0
     if not fits:
         return on_device_plain(green_guess, green_free, retarded, momentum_order)
-    cosine, sine = small_tables(momentum_order, count, L1)
-    _, sigma, late = born_call(n, green_guess[0], cosine, sine, L1)
+    _, sigma, late = born_call(n, green_guess[0], momentum_order.astype(jnp.int32)[None], L1)
     pieces = lax.all_to_all(late, "mom", split_axis=0, concat_axis=0, tiled=True)
     green, sigma = dyson_early(sigma, retarded, green_free[0])
     green, sigma = dyson_late(pieces, retarded, green_free[0], green, sigma)

time: 841 us -> 836 us (level)
  no operation moved by 1% of the time
where the time goes in v4:
time: 836 us
  Pallas kernels  794 us (95%)
  starting transfers between devices  31.5 us (4%)
  waiting for transfers between devices  9.45 us (1%)
    pallas_call x1, Pallas kernels, born_call(): pl.pallas_call(functools.partial(born_kernel, n, chunks, first_len), out_...  742 us
    pallas_call x1, Pallas kernels, dyson_early(): pl.pallas_call(dyson_early_kernel, grid=(early // step,), in_specs=[spec]...  43.4 us
    all_to_all x1, starting transfers between devices, on_device(): lax.all_to_all(late, 'mom', split_axis=0, concat_axis=0, tiled=True)  31.5 us
  transfers between devices with their start and end apart: 1, of which 1 were waited for; matrix products, arithmetic and copies ran while one was open for 0% of the time, Pallas kernels for 5%

profile of v4, /device:TPU:0, one launch (start us, length us, event | category | flops | bytes accessed | tf_op | source)
XLA Modules:
  0.0 835.9 jit_solution(8210130295452997714)
XLA Ops:
  0.6 742.3 %born.1 = (f32[3,512,8,384]{3,2,1,0:T(8,128)}, f32[56,192,384]{2,1,0:T(8,128)}, f32[8,8,24,384]{3,2,1,0:T(8,128)}) custom-call(f32[64,192,384]{2,1,0:T(8,128)} %bitcast.5, s32[1,512]{1,0:T(1,128)} %bitcast.10), custom_call_target="tpu_custom_call" | custom-call | tf_op jit(solution)/shard_map/born/pallas_call | solution.py:549
  743.0 31.5 %all-to-all-start = ((f32[8,8,24,384]{3,2,1,0:T(8,128)}), f32[8,8,24,384]{3,2,1,0:T(8,128)S(1)}, u32[]{:S(2)}, u32[]{:S(2)}) async-start(f32[8,8,24,384]{3,2,1,0:T(8,128)} %get-tuple-element.8), calls=%async_computation | async-start | bytes 4718592 | tf_op jit(solution)/shard_map/all_to_all | solution.py:592
  774.5 43.4 %dyson_early.1 = (f32[64,192,384]{2,1,0:T(8,128)}, f32[64,192,384]{2,1,0:T(8,128)}) custom-call(f32[56,192,384]{2,1,0:T(8,128)} %get-tuple-element.9.sig_ref, f32[64,192,384]{2,1,0:T(8,128)} %ret_ref.3, f32[64,192,384]{2,1,0:T(8,128)} %bitcast.6), custom_call_target="tpu_custom_call" | custom-call | flops 19025362944 | bytes 82575360 | tf_op jit(solution)/shard_map/dyson_early/pallas_call | solution.py:240
  817.9 9.4 %all-to-all-done.sig_ref = f32[8,8,24,384]{3,2,1,0:T(8,128)S(1)} async-done(((f32[8,8,24,384]{3,2,1,0:T(8,128)}), f32[8,8,24,384]{3,2,1,0:T(8,128)S(1)}, u32[]{:S(2)}, u32[]{:S(2)}) %all-to-all-start) | async-done | bytes 2359328 | tf_op jit(solution)/shard_map/all_to_all | solution.py:592
  827.4 8.5 %dyson_late.1 = (f32[64,192,384]{2,1,0:T(8,128)}, f32[64,192,384]{2,1,0:T(8,128)}) custom-call(f32[8,8,24,384]{3,2,1,0:T(8,128)S(1)} %all-to-all-done.sig_ref, f32[64,192,384]{2,1,0:T(8,128)} %ret_ref.3, f32[64,192,384]{2,1,0:T(8,128)} %bitcast.7, f32[64,192,384]{2,1,0:T(8,128)} %get-tuple-element.10._green, ...), custom_call_target="tpu_custom_call", output_to_operand_aliasing={{0}: (3, {}), {1}: (4, {})} | custom-call | flops 2717908992 | bytes 11796480 | tf_op jit(solution)/shard_map/dyson_late/pallas_call | solution.py:260
Async XLA Ops:
  743.0 84.4 %all-to-all-start = ((f32[8,8,24,384]{3,2,1,0:T(8,128)}), f32[8,8,24,384]{3,2,1,0:T(8,128)S(1)}, u32[]{:S(2)}, u32[]{:S(2)}) async-start(f32[8,8,24,384]{3,2,1,0:T(8,128)} %get-tuple-element.8), calls=%async_computation | async-start | bytes 4718592 | tf_op jit(solution)/shard_map/all_to_all | solution.py:592
